TPU v7x, 512 devices: a whole 4x4x16 slice. The times are simulated.
512 devices in a mesh: leaf: 32 (over z, core), front: 16 (over y, x).
Axes of the slice: x: 4, y: 4, z: 16, core: 2. Of those that a mesh axis runs over, the one named last changes fastest.
Arguments:
- forcing: bfloat16 [32, 10240, 128], P('leaf', 'front'), may hold values from -6 to 6
- live: int32 [2, 32], replicated, may hold values from 40 to 80, as said below
- lower_inv: bfloat16 [32, 10240, 960], P('leaf', 'front'), may hold values from -0.0625 to 0.0625
- lower_upd: bfloat16 [32, 10240, 640], P('leaf', 'front'), may hold values from -0.0625 to 0.0625
- upper_inv: bfloat16 [32, 10240, 960], P('leaf', 'front'), may hold values from -0.0625 to 0.0625
- upper_upd: bfloat16 [32, 10240, 640], P('leaf', 'front'), may hold values from -0.0625 to 0.0625
Outputs:
- solution: bfloat16 [2, 32, 10240, 128], P(None, 'leaf', 'front')
Inputs may be any that keep to these rules, and one draw needn't show every extreme that they name: Entries (l, j) with j at or beyond 2**(1 - l) are not read. The root's separator is live in full.
All inputs are finite; a program needn't handle non-finite values.
Results may differ from a plain program's by a relative error of at most 0.008.
Values may be sent and summed in bfloat16 or wider, within the bound.
No kernel may reach another device: no remote copies, remote signals or barrier semaphores. Data moves between devices by JAX's collectives and lax.ppermute only.
A program may use at most 64 MiB of HBM per device.

v0:
```python
import jax
import jax.numpy as jnp
from jax import lax
from jax.sharding import PartitionSpec as P

BLK = 128
LEV = 2


def from_root(array, axis, root):
    mine = lax.axis_index(axis) == root
    return lax.psum(jnp.where(mine, array, jnp.zeros_like(array)), axis)


def partner(block, axis, bit):
    count = lax.axis_size(axis)
    route = []
    for low in range(count):
        high = low | 1 << bit
        if high != low and high < count:
            route += [(low, high), (high, low)]
    return lax.ppermute(block, axis, route)


def body(forcing, live, lower_inv, lower_upd, upper_inv, upper_upd):
    n_leaf = lax.axis_size("leaf")
    sep_dev = forcing.shape[1]
    n_rhs = forcing.shape[2]
    sep = sep_dev * lax.axis_size("front")
    skip = n_leaf.bit_length() - LEV
    leaf_id = lax.axis_index("leaf")
    front_id = lax.axis_index("front")
    rows = front_id * sep_dev + jnp.arange(sep_dev)
    first = 2 * (sep >> skip)

    def level_mask(level):
        count = live[level][leaf_id >> level + skip]
        return (rows < count * BLK).astype(jnp.float32)[:, None]

    def fetch(block, level, residual_kind):
        depth = level + skip
        width = sep >> depth
        start = (leaf_id & (1 << depth) - 1) * width
        owner = start // sep_dev
        if residual_kind:
            piece = from_root(block, "front", owner)
        else:
            piece = from_root(block, "front", owner)
        return lax.dynamic_slice_in_dim(piece, start % sep_dev, width, 0)

    def subtree_total(partial_value, depth):
        for bit in range(depth):
            partial_value = partial_value + partner(partial_value, "leaf", bit)
        return partial_value

    residual = subtree_total(forcing[0].astype(jnp.float32), skip)
    forward = []
    for level in range(LEV):
        depth = level + skip
        width = sep >> depth
        offset = first - 2 * width
        mask = level_mask(level)
        masked = (mask * residual).astype(jnp.bfloat16)
        picked = fetch(masked, level, True)
        y_term = jnp.dot(
            lower_inv[0, :, offset : offset + width], picked, preferred_element_type=jnp.float32
        )
        if level < LEV - 1:
            c_term = jnp.dot(
                lower_upd[0, :, offset : offset + width], picked, preferred_element_type=jnp.float32
            )
            summed = subtree_total(jnp.concatenate([y_term, -c_term], 0), depth)
            y_sum = summed[:sep_dev]
            loads = summed[sep_dev:]
            residual = loads + partner(loads, "leaf", depth)
        else:
            y_sum = subtree_total(y_term, depth)
        forward.append((mask * y_sum).astype(jnp.bfloat16))
    results = [None] * LEV
    above = None
    for level in reversed(range(LEV)):
        depth = level + skip
        width = sep >> depth
        offset = first - 2 * width
        mask = level_mask(level)
        if above is None:
            picked = fetch(forward[level], level, False)
            term = jnp.dot(
                upper_inv[0, :, offset : offset + width], picked, preferred_element_type=jnp.float32
            )
        else:
            picked = fetch(jnp.concatenate([forward[level], above], 1), level, False)
            term = jnp.dot(
                upper_inv[0, :, offset : offset + width],
                picked[:, :n_rhs],
                preferred_element_type=jnp.float32,
            )
            term = term - jnp.dot(
                upper_upd[0, :, offset : offset + width],
                picked[:, n_rhs:],
                preferred_element_type=jnp.float32,
            )
        solved = (mask * subtree_total(term, depth)).astype(jnp.bfloat16)
        results[level] = solved
        above = solved
    return jnp.stack(results)[:, None]


def solution(mesh):
    return jax.shard_map(
        body,
        mesh=mesh,
        in_specs=(
            P("leaf", "front", None),
            P(),
            P("leaf", "front", None),
            P("leaf", "front", None),
            P("leaf", "front", None),
            P("leaf", "front", None),
        ),
        out_specs=P(None, "leaf", "front", None),
        check_vma=False,
    )
```

profile of v0, /device:TPU:1, one launch (start us, length us, event | category | flops | bytes accessed | tf_op | source)
XLA Modules:
  0.0 972.4 jit_solution(18222243295650057958)
XLA Ops:
  7.7 8.8 collective-permute-start
  17.8 1.9 collective-permute-start.1
  19.7 8.9 collective-permute-done.1
  28.7 2.1 collective-permute-start.2
  30.7 17.4 %collective-permute-done.2 = f32[640,128]{0,1:T(8,128)S(1)} collective-permute-done((f32[640,128]{0,1:T(8,128)S(1)}, f32[640,128]{0,1:T(8,128)S(1)}, u32[]{:S(2)}, u32[]{:S(2)}) %collective-permute-start.2) | collective-permute-done | bytes 327712 | tf_op jit(solution)/shard_map/ppermute | solution.py:22
  48.2 3.5 collective-permute-start.3
  53.1 29.1 %collective-permute-done.3 = f32[640,128]{0,1:T(8,128)S(1)} collective-permute-done((f32[640,128]{0,1:T(8,128)S(1)}, f32[640,128]{0,1:T(8,128)S(1)}, u32[]{:S(2)}, u32[]{:S(2)}) %collective-permute-start.3) | collective-permute-done | bytes 327712 | tf_op jit(solution)/shard_map/ppermute | solution.py:22
  82.9 112.0 %all-reduce.5.cloned.1.call-done = bf16[640,128]{0,1:T(8,128)(2,1)} async-done(((bf16[640,128]{0,1:T(8,128)(2,1)}), bf16[640,128]{0,1:T(8,128)(2,1)}) %all-reduce.5.cloned.1.call-update) | async-done | bytes 163856 | tf_op jit(solution)/shard_map/psum | solution.py:12
  194.9 1.3 convolution_bitcast_fusion.2
  196.7 4.4 collective-permute-start.4
  201.1 1.7 collective-permute-done.4
  202.9 3.2 collective-permute-start.5
  206.1 14.7 %collective-permute-done.5 = f32[1280,128]{0,1:T(8,128)S(1)} collective-permute-done((f32[1280,128]{0,1:T(8,128)S(1)}, f32[1280,128]{0,1:T(8,128)S(1)}, u32[]{:S(2)}, u32[]{:S(2)}) %collective-permute-start.5) | collective-permute-done | bytes 655392 | tf_op jit(solution)/shard_map/ppermute | solution.py:22
  220.8 4.2 collective-permute-start.6
  225.0 28.3 %collective-permute-done.6 = f32[1280,128]{0,1:T(8,128)S(1)} collective-permute-done((f32[1280,128]{0,1:T(8,128)S(1)}, f32[1280,128]{0,1:T(8,128)S(1)}, u32[]{:S(2)}, u32[]{:S(2)}) %collective-permute-start.6) | collective-permute-done | bytes 655392 | tf_op jit(solution)/shard_map/ppermute | solution.py:22
  253.3 7.4 collective-permute-start.7
  260.7 63.4 %collective-permute-done.7 = f32[1280,128]{0,1:T(8,128)S(1)} collective-permute-done((f32[1280,128]{0,1:T(8,128)S(1)}, f32[1280,128]{0,1:T(8,128)S(1)}, u32[]{:S(2)}, u32[]{:S(2)}) %collective-permute-start.7) | collective-permute-done | bytes 655392 | tf_op jit(solution)/shard_map/ppermute | solution.py:22
  324.2 11.1 %collective-permute-start.8 = (f32[640,128]{0,1:T(8,128)S(1)}, f32[640,128]{0,1:T(8,128)S(1)}, u32[]{:S(2)}, u32[]{:S(2)}) collective-permute-start(f32[640,128]{0,1:T(8,128)S(1)} %get-tuple-element.6), channel_id=1, source_target_pairs={{0,256},{256,0},{16,272},{272,16},{32,288},{288,32},{48,304},{304,... | collective-permute-start | bytes 983048 | tf_op jit(solution)/shard_map/ppermute | solution.py:22
  336.0 12.4 %collective-permute-done.8 = f32[640,128]{0,1:T(8,128)S(1)} collective-permute-done((f32[640,128]{0,1:T(8,128)S(1)}, f32[640,128]{0,1:T(8,128)S(1)}, u32[]{:S(2)}, u32[]{:S(2)}) %collective-permute-start.8) | collective-permute-done | bytes 327712 | tf_op jit(solution)/shard_map/ppermute | solution.py:22
  349.2 113.3 %all-reduce.7.cloned.1.call-done = bf16[640,128]{0,1:T(8,128)(2,1)} async-done(((bf16[640,128]{0,1:T(8,128)(2,1)}), bf16[640,128]{0,1:T(8,128)(2,1)}) %all-reduce.7.cloned.1.call-update) | async-done | bytes 163856 | tf_op jit(solution)/shard_map/psum | solution.py:12
  463.7 4.4 collective-permute-start.9
  469.4 3.2 collective-permute-start.10
  472.6 7.6 collective-permute-done.10
  480.3 4.2 collective-permute-start.11
  484.5 14.2 %collective-permute-done.11 = f32[640,128]{0,1:T(8,128)S(1)} collective-permute-done((f32[640,128]{0,1:T(8,128)S(1)}, f32[640,128]{0,1:T(8,128)S(1)}, u32[]{:S(2)}, u32[]{:S(2)}) %collective-permute-start.11) | collective-permute-done | bytes 327712 | tf_op jit(solution)/shard_map/ppermute | solution.py:22
  498.7 7.5 collective-permute-start.12
  506.2 28.2 %collective-permute-done.12 = f32[640,128]{0,1:T(8,128)S(1)} collective-permute-done((f32[640,128]{0,1:T(8,128)S(1)}, f32[640,128]{0,1:T(8,128)S(1)}, u32[]{:S(2)}, u32[]{:S(2)}) %collective-permute-start.12) | collective-permute-done | bytes 327712 | tf_op jit(solution)/shard_map/ppermute | solution.py:22
  534.5 18.2 %collective-permute-start.13 = (f32[640,128]{0,1:T(8,128)S(1)}, f32[640,128]{0,1:T(8,128)S(1)}, u32[]{:S(2)}, u32[]{:S(2)}) collective-permute-start(f32[640,128]{0,1:T(8,128)S(1)} %add.131), channel_id=1, source_target_pairs={{0,256},{256,0},{16,272},{272,16},{32,288},{288,32},{48,304},{304,... | collective-permute-start | bytes 983048 | tf_op jit(solution)/shard_map/ppermute | solution.py:22
  552.7 14.1 %collective-permute-done.13 = f32[640,128]{0,1:T(8,128)S(1)} collective-permute-done((f32[640,128]{0,1:T(8,128)S(1)}, f32[640,128]{0,1:T(8,128)S(1)}, u32[]{:S(2)}, u32[]{:S(2)}) %collective-permute-start.13) | collective-permute-done | bytes 327712 | tf_op jit(solution)/shard_map/ppermute | solution.py:22
  567.6 110.0 %all-reduce.9.cloned.1.call-done = bf16[640,128]{0,1:T(8,128)(2,1)} async-done(((bf16[640,128]{0,1:T(8,128)(2,1)}), bf16[640,128]{0,1:T(8,128)(2,1)}) %all-reduce.9.cloned.1.call-update) | async-done | bytes 163856 | tf_op jit(solution)/shard_map/psum | solution.py:12
  678.8 4.4 collective-permute-start.14
  684.5 3.2 collective-permute-start.15
  687.7 7.6 collective-permute-done.15
  695.3 4.2 collective-permute-start.16
  699.5 14.2 %collective-permute-done.16 = f32[640,128]{0,1:T(8,128)S(1)} collective-permute-done((f32[640,128]{0,1:T(8,128)S(1)}, f32[640,128]{0,1:T(8,128)S(1)}, u32[]{:S(2)}, u32[]{:S(2)}) %collective-permute-start.16) | collective-permute-done | bytes 327712 | tf_op jit(solution)/shard_map/ppermute | solution.py:22
  713.7 7.4 collective-permute-start.17
  721.1 28.2 %collective-permute-done.17 = f32[640,128]{0,1:T(8,128)S(1)} collective-permute-done((f32[640,128]{0,1:T(8,128)S(1)}, f32[640,128]{0,1:T(8,128)S(1)}, u32[]{:S(2)}, u32[]{:S(2)}) %collective-permute-start.17) | collective-permute-done | bytes 327712 | tf_op jit(solution)/shard_map/ppermute | solution.py:22
  749.4 18.2 %collective-permute-start.18 = (f32[640,128]{0,1:T(8,128)S(1)}, f32[640,128]{0,1:T(8,128)S(1)}, u32[]{:S(2)}, u32[]{:S(2)}) collective-permute-start(f32[640,128]{0,1:T(8,128)S(1)} %add.136), channel_id=1, source_target_pairs={{0,256},{256,0},{16,272},{272,16},{32,288},{288,32},{48,304},{304,... | collective-permute-start | bytes 983048 | tf_op jit(solution)/shard_map/ppermute | solution.py:22
  767.6 14.1 %collective-permute-done.18 = f32[640,128]{0,1:T(8,128)S(1)} collective-permute-done((f32[640,128]{0,1:T(8,128)S(1)}, f32[640,128]{0,1:T(8,128)S(1)}, u32[]{:S(2)}, u32[]{:S(2)}) %collective-permute-start.18) | collective-permute-done | bytes 327712 | tf_op jit(solution)/shard_map/ppermute | solution.py:22
  782.6 110.6 %all-reduce.11.cloned.1.call-done = bf16[640,256]{0,1:T(8,128)(2,1)} async-done(((bf16[640,256]{0,1:T(8,128)(2,1)}), bf16[640,256]{0,1:T(8,128)(2,1)}) %all-reduce.11.cloned.1.call-update) | async-done | bytes 327696 | tf_op jit(solution)/shard_map/psum | solution.py:12
  893.2 1.3 fusion.3
  894.9 3.9 collective-permute-start.19
  900.1 3.2 collective-permute-start.20
  903.2 7.6 collective-permute-done.20
  910.9 4.2 collective-permute-start.21
  915.1 14.2 %collective-permute-done.21 = f32[640,128]{0,1:T(8,128)S(1)} collective-permute-done((f32[640,128]{0,1:T(8,128)S(1)}, f32[640,128]{0,1:T(8,128)S(1)}, u32[]{:S(2)}, u32[]{:S(2)}) %collective-permute-start.21) | collective-permute-done | bytes 327712 | tf_op jit(solution)/shard_map/ppermute | solution.py:22
  929.3 7.4 collective-permute-start.22
  936.7 28.2 %collective-permute-done.22 = f32[640,128]{0,1:T(8,128)S(1)} collective-permute-done((f32[640,128]{0,1:T(8,128)S(1)}, f32[640,128]{0,1:T(8,128)S(1)}, u32[]{:S(2)}, u32[]{:S(2)}) %collective-permute-start.22) | collective-permute-done | bytes 327712 | tf_op jit(solution)/shard_map/ppermute | solution.py:22
  (64 shorter events, 16.2 us)
Async XLA Ops:
  6.5 189.7 %copy-start = (bf16[1,640,640]{2,1,0:T(8,128)(2,1)S(1)}, bf16[1,640,640]{2,1,0:T(8,128)(2,1)}, u32[]{:S(2)}) copy-start(bf16[1,640,640]{2,1,0:T(8,128)(2,1)} %param.9) | copy-start | bytes 2457604
  6.5 188.4 %all-reduce.5.cloned.1.call-start = ((), (), s32[]{:S(2)}) async-start(), calls=%async_computation | async-start | bytes 327680 | tf_op jit(solution)/shard_map/psum | solution.py:12
  7.7 44.0 %copy-start.6 = (s32[2,32]{1,0:T(2,128)S(1)}, s32[2,32]{1,0:T(2,128)}, u32[]{:S(2)}) copy-start(s32[2,32]{1,0:T(2,128)} %param.7) | copy-start | bytes 772
  7.7 10.0 %collective-permute-start = (f32[640,128]{0,1:T(8,128)S(1)}, f32[640,128]{0,1:T(8,128)S(1)}, u32[]{:S(2)}, u32[]{:S(2)}) collective-permute-start(f32[640,128]{0,1:T(8,128)S(1)} %bitcast_convert_fusion), channel_id=1, source_target_pairs={{0,16},{16,0},{32,48},{48,32},{64,80},{80,64},{96,112},{112,96},{1... | collective-permute-start | bytes 983048 | tf_op jit(solution)/shard_map/ppermute | solution.py:22
  17.8 10.8 %collective-permute-start.1 = (f32[640,128]{0,1:T(8,128)S(1)}, f32[640,128]{0,1:T(8,128)S(1)}, u32[]{:S(2)}, u32[]{:S(2)}) collective-permute-start(f32[640,128]{0,1:T(8,128)S(1)} %fusion.22), channel_id=1, source_target_pairs={{0,32},{32,0},{16,48},{48,16},{64,96},{96,64},{80,112},{112,80},{1... | collective-permute-start | bytes 983048 | tf_op jit(solution)/shard_map/ppermute | solution.py:22
  28.6 166.3 %copy-start.1 = (bf16[1,640,960]{1,2,0:T(8,128)(2,1)S(1)}, bf16[1,640,960]{1,2,0:T(8,128)(2,1)}, u32[]{:S(2)}) copy-start(bf16[1,640,960]{1,2,0:T(8,128)(2,1)} %param.8) | copy-start | bytes 3686404
  28.7 19.5 %collective-permute-start.2 = (f32[640,128]{0,1:T(8,128)S(1)}, f32[640,128]{0,1:T(8,128)S(1)}, u32[]{:S(2)}, u32[]{:S(2)}) collective-permute-start(f32[640,128]{0,1:T(8,128)S(1)} %add.117), channel_id=1, source_target_pairs={{0,64},{64,0},{16,80},{80,16},{32,96},{96,32},{48,112},{112,48},{1... | collective-permute-start | bytes 983048 | tf_op jit(solution)/shard_map/ppermute | solution.py:22
  48.2 33.9 %collective-permute-start.3 = (f32[640,128]{0,1:T(8,128)S(1)}, f32[640,128]{0,1:T(8,128)S(1)}, u32[]{:S(2)}, u32[]{:S(2)}) collective-permute-start(f32[640,128]{0,1:T(8,128)S(1)} %add.118), channel_id=1, source_target_pairs={{0,128},{128,0},{16,144},{144,16},{32,160},{160,32},{48,176},{176,... | collective-permute-start | bytes 983048 | tf_op jit(solution)/shard_map/ppermute | solution.py:22
  82.9 379.7 %all-reduce.7.cloned.1.call-start = ((), (), s32[]{:S(2)}) async-start(), calls=%async_computation.1 | async-start | bytes 327680 | tf_op jit(solution)/shard_map/psum | solution.py:12
  194.9 1.3 copy-start.4
  196.7 6.1 collective-permute-start.4
  202.9 17.8 %collective-permute-start.5 = (f32[1280,128]{0,1:T(8,128)S(1)}, f32[1280,128]{0,1:T(8,128)S(1)}, u32[]{:S(2)}, u32[]{:S(2)}) collective-permute-start(f32[1280,128]{0,1:T(8,128)S(1)} %fusion.29), channel_id=1, source_target_pairs={{0,32},{32,0},{16,48},{48,16},{64,96},{96,64},{80,112},{112,80},{1... | collective-permute-start | bytes 1966088 | tf_op jit(solution)/shard_map/ppermute | solution.py:22
  220.8 32.4 %collective-permute-start.6 = (f32[1280,128]{0,1:T(8,128)S(1)}, f32[1280,128]{0,1:T(8,128)S(1)}, u32[]{:S(2)}, u32[]{:S(2)}) collective-permute-start(f32[1280,128]{0,1:T(8,128)S(1)} %add.121), channel_id=1, source_target_pairs={{0,64},{64,0},{16,80},{80,16},{32,96},{96,32},{48,112},{112,48},{1... | collective-permute-start | bytes 1966088 | tf_op jit(solution)/shard_map/ppermute | solution.py:22
  253.3 70.8 %collective-permute-start.7 = (f32[1280,128]{0,1:T(8,128)S(1)}, f32[1280,128]{0,1:T(8,128)S(1)}, u32[]{:S(2)}, u32[]{:S(2)}) collective-permute-start(f32[1280,128]{0,1:T(8,128)S(1)} %add.122), channel_id=1, source_target_pairs={{0,128},{128,0},{16,144},{144,16},{32,160},{160,32},{48,176},{176,... | collective-permute-start | bytes 1966088 | tf_op jit(solution)/shard_map/ppermute | solution.py:22
  324.2 24.2 %collective-permute-start.8 = (f32[640,128]{0,1:T(8,128)S(1)}, f32[640,128]{0,1:T(8,128)S(1)}, u32[]{:S(2)}, u32[]{:S(2)}) collective-permute-start(f32[640,128]{0,1:T(8,128)S(1)} %get-tuple-element.6), channel_id=1, source_target_pairs={{0,256},{256,0},{16,272},{272,16},{32,288},{288,32},{48,304},{304,... | collective-permute-start | bytes 983048 | tf_op jit(solution)/shard_map/ppermute | solution.py:22
  349.1 328.4 %all-reduce.9.cloned.1.call-start = ((), (), s32[]{:S(2)}) async-start(), calls=%async_computation.2 | async-start | bytes 327680 | tf_op jit(solution)/shard_map/psum | solution.py:12
  463.7 5.7 collective-permute-start.9
  469.4 10.8 %collective-permute-start.10 = (f32[640,128]{0,1:T(8,128)S(1)}, f32[640,128]{0,1:T(8,128)S(1)}, u32[]{:S(2)}, u32[]{:S(2)}) collective-permute-start(f32[640,128]{0,1:T(8,128)S(1)} %add.128), channel_id=1, source_target_pairs={{0,32},{32,0},{16,48},{48,16},{64,96},{96,64},{80,112},{112,80},{1... | collective-permute-start | bytes 983048 | tf_op jit(solution)/shard_map/ppermute | solution.py:22
  480.3 18.4 %collective-permute-start.11 = (f32[640,128]{0,1:T(8,128)S(1)}, f32[640,128]{0,1:T(8,128)S(1)}, u32[]{:S(2)}, u32[]{:S(2)}) collective-permute-start(f32[640,128]{0,1:T(8,128)S(1)} %add.129), channel_id=1, source_target_pairs={{0,64},{64,0},{16,80},{80,16},{32,96},{96,32},{48,112},{112,48},{1... | collective-permute-start | bytes 983048 | tf_op jit(solution)/shard_map/ppermute | solution.py:22
  498.7 178.9 %copy-start.2 = (bf16[1,640,960]{1,2,0:T(8,128)(2,1)S(1)}, bf16[1,640,960]{1,2,0:T(8,128)(2,1)}, u32[]{:S(2)}) copy-start(bf16[1,640,960]{1,2,0:T(8,128)(2,1)} %param.10) | copy-start | bytes 3686404
  498.7 35.7 %collective-permute-start.12 = (f32[640,128]{0,1:T(8,128)S(1)}, f32[640,128]{0,1:T(8,128)S(1)}, u32[]{:S(2)}, u32[]{:S(2)}) collective-permute-start(f32[640,128]{0,1:T(8,128)S(1)} %add.130), channel_id=1, source_target_pairs={{0,128},{128,0},{16,144},{144,16},{32,160},{160,32},{48,176},{176,... | collective-permute-start | bytes 983048 | tf_op jit(solution)/shard_map/ppermute | solution.py:22
  534.5 32.3 %collective-permute-start.13 = (f32[640,128]{0,1:T(8,128)S(1)}, f32[640,128]{0,1:T(8,128)S(1)}, u32[]{:S(2)}, u32[]{:S(2)}) collective-permute-start(f32[640,128]{0,1:T(8,128)S(1)} %add.131), channel_id=1, source_target_pairs={{0,256},{256,0},{16,272},{272,16},{32,288},{288,32},{48,304},{304,... | collective-permute-start | bytes 983048 | tf_op jit(solution)/shard_map/ppermute | solution.py:22
  567.5 325.7 %all-reduce.11.cloned.1.call-start = ((), (), s32[]{:S(2)}) async-start(), calls=%async_computation.3 | async-start | bytes 655360 | tf_op jit(solution)/shard_map/psum | solution.py:12
  678.8 5.7 collective-permute-start.14
  684.5 10.8 %collective-permute-start.15 = (f32[640,128]{0,1:T(8,128)S(1)}, f32[640,128]{0,1:T(8,128)S(1)}, u32[]{:S(2)}, u32[]{:S(2)}) collective-permute-start(f32[640,128]{0,1:T(8,128)S(1)} %add.133), channel_id=1, source_target_pairs={{0,32},{32,0},{16,48},{48,16},{64,96},{96,64},{80,112},{112,80},{1... | collective-permute-start | bytes 983048 | tf_op jit(solution)/shard_map/ppermute | solution.py:22
  695.3 18.4 %collective-permute-start.16 = (f32[640,128]{0,1:T(8,128)S(1)}, f32[640,128]{0,1:T(8,128)S(1)}, u32[]{:S(2)}, u32[]{:S(2)}) collective-permute-start(f32[640,128]{0,1:T(8,128)S(1)} %add.134), channel_id=1, source_target_pairs={{0,64},{64,0},{16,80},{80,16},{32,96},{96,32},{48,112},{112,48},{1... | collective-permute-start | bytes 983048 | tf_op jit(solution)/shard_map/ppermute | solution.py:22
  713.7 35.6 %collective-permute-start.17 = (f32[640,128]{0,1:T(8,128)S(1)}, f32[640,128]{0,1:T(8,128)S(1)}, u32[]{:S(2)}, u32[]{:S(2)}) collective-permute-start(f32[640,128]{0,1:T(8,128)S(1)} %add.135), channel_id=1, source_target_pairs={{0,128},{128,0},{16,144},{144,16},{32,160},{160,32},{48,176},{176,... | collective-permute-start | bytes 983048 | tf_op jit(solution)/shard_map/ppermute | solution.py:22
  749.4 32.3 %collective-permute-start.18 = (f32[640,128]{0,1:T(8,128)S(1)}, f32[640,128]{0,1:T(8,128)S(1)}, u32[]{:S(2)}, u32[]{:S(2)}) collective-permute-start(f32[640,128]{0,1:T(8,128)S(1)} %add.136), channel_id=1, source_target_pairs={{0,256},{256,0},{16,272},{272,16},{32,288},{288,32},{48,304},{304,... | collective-permute-start | bytes 983048 | tf_op jit(solution)/shard_map/ppermute | solution.py:22
  781.7 112.8 %copy-start.3 = (bf16[1,640,640]{2,1,0:T(8,128)(2,1)S(1)}, bf16[1,640,640]{2,1,0:T(8,128)(2,1)}, u32[]{:S(2)}) copy-start(bf16[1,640,640]{2,1,0:T(8,128)(2,1)} %param.11) | copy-start | bytes 2457604
  893.2 1.3 copy-start.5
  894.9 5.1 collective-permute-start.19
  900.1 10.8 %collective-permute-start.20 = (f32[640,128]{0,1:T(8,128)S(1)}, f32[640,128]{0,1:T(8,128)S(1)}, u32[]{:S(2)}, u32[]{:S(2)}) collective-permute-start(f32[640,128]{0,1:T(8,128)S(1)} %add.138), channel_id=1, source_target_pairs={{0,32},{32,0},{16,48},{48,16},{64,96},{96,64},{80,112},{112,80},{1... | collective-permute-start | bytes 983048 | tf_op jit(solution)/shard_map/ppermute | solution.py:22
  910.9 18.4 %collective-permute-start.21 = (f32[640,128]{0,1:T(8,128)S(1)}, f32[640,128]{0,1:T(8,128)S(1)}, u32[]{:S(2)}, u32[]{:S(2)}) collective-permute-start(f32[640,128]{0,1:T(8,128)S(1)} %add.139), channel_id=1, source_target_pairs={{0,64},{64,0},{16,80},{80,16},{32,96},{96,32},{48,112},{112,48},{1... | collective-permute-start | bytes 983048 | tf_op jit(solution)/shard_map/ppermute | solution.py:22
  929.3 35.6 %collective-permute-start.22 = (f32[640,128]{0,1:T(8,128)S(1)}, f32[640,128]{0,1:T(8,128)S(1)}, u32[]{:S(2)}, u32[]{:S(2)}) collective-permute-start(f32[640,128]{0,1:T(8,128)S(1)} %add.140), channel_id=1, source_target_pairs={{0,128},{128,0},{16,144},{144,16},{32,160},{160,32},{48,176},{176,... | collective-permute-start | bytes 983048 | tf_op jit(solution)/shard_map/ppermute | solution.py:22
Sparse Core Ops, SparseCore 0:
  83.0 111.9 all-reduce.4
  349.3 113.2 all-reduce.6
  567.7 109.8 all-reduce.8
  782.7 110.4 all-reduce.10
where the time goes:
time: 973 us; the launch traced here: 972 us
  waiting for transfers between devices  805 us (83%)
  starting transfers between devices  140 us (14%)
  between operations  13.6 us (1%)
    psum x4, waiting for transfers between devices, from_root(): return lax.psum(jnp.where(mine, array, jnp.zeros_like(array)), axis)  446 us
    ppermute x23, waiting for transfers between devices, partner(): return lax.ppermute(block, axis, route)  359 us
    ppermute x23, starting transfers between devices, partner(): return lax.ppermute(block, axis, route)  140 us
  transfers between devices with their start and end apart: 27, of which 27 were waited for; matrix products, arithmetic and copies ran while one was open for 0% of the time, Pallas kernels for 0%

commit v1 on v0

--- a/solution.py
+++ b/solution.py
@@ -7,9 +7,15 @@
 LEV = 2
 
 
+def gather_and_add(value, name):
+    pieces = lax.all_gather(value, name, axis=0, tiled=False)
+    result = pieces.sum(axis=0)
+    return result
+
+
 def from_root(array, axis, root):
     mine = lax.axis_index(axis) == root
-    return lax.psum(jnp.where(mine, array, jnp.zeros_like(array)), axis)
+    return gather_and_add(jnp.where(mine, array, jnp.zeros_like(array)), axis)
 
 
 def partner(block, axis, bit):

time: 973 us -> 786 us (0.81)
  waiting for transfers between devices: 805 us -> 610 us
    psum x4 -> x0, waiting for transfers between devices: 446 us -> none  [from_root(): return lax.psum(jnp.where(mine, array, jnp.zeros_like(array)), axis)]
    all_gather x0 -> x4, waiting for transfers between devices: none -> 251 us  [gather_and_add(): pieces = lax.all_gather(value, name, axis=0, tiled=False)]
where the time goes in v1:
time: 786 us; the launch traced here: 785 us
  waiting for transfers between devices  610 us (78%)
  starting transfers between devices  138 us (18%)
  between operations  13.7 us (2%)
  other arithmetic  12.2 us (2%)
  local copies, waits for them, and re-layouts  9.65 us (1%)
    ppermute x23, waiting for transfers between devices, partner(): return lax.ppermute(block, axis, route)  359 us
    all_gather x4, waiting for transfers between devices, gather_and_add(): pieces = lax.all_gather(value, name, axis=0, tiled=False)  251 us
    ppermute x23, starting transfers between devices, partner(): return lax.ppermute(block, axis, route)  137 us
  transfers between devices with their start and end apart: 27, of which 27 were waited for; matrix products, arithmetic and copies ran while one was open for 0% of the time, Pallas kernels for 0%

profile of v1, /device:TPU:1, one launch (start us, length us, event | category | flops | bytes accessed | tf_op | source)
XLA Modules:
  0.0 784.9 jit_solution(10403242534536177562)
XLA Ops:
  7.7 8.8 %collective-permute-start = (f32[640,128]{0,1:T(8,128)S(1)}, f32[640,128]{0,1:T(8,128)S(1)}, u32[]{:S(2)}, u32[]{:S(2)}) collective-permute-start(f32[640,128]{0,1:T(8,128)S(1)} %bitcast_convert_fusion), channel_id=1, source_target_pairs={{0,16},{16,0},{32,48},{48,32},{64,80},{80,64},{96,112},{112,96},{1... | collective-permute-start | bytes 983048 | tf_op jit(solution)/shard_map/ppermute | solution.py:28
  19.7 8.9 %collective-permute-done.1 = f32[640,128]{0,1:T(8,128)S(1)} collective-permute-done((f32[640,128]{0,1:T(8,128)S(1)}, f32[640,128]{0,1:T(8,128)S(1)}, u32[]{:S(2)}, u32[]{:S(2)}) %collective-permute-start.1) | collective-permute-done | bytes 327712 | tf_op jit(solution)/shard_map/ppermute | solution.py:28
  28.6 1.9 collective-permute-start.2
  30.6 17.4 %collective-permute-done.2 = f32[640,128]{0,1:T(8,128)S(1)} collective-permute-done((f32[640,128]{0,1:T(8,128)S(1)}, f32[640,128]{0,1:T(8,128)S(1)}, u32[]{:S(2)}, u32[]{:S(2)}) %collective-permute-start.2) | collective-permute-done | bytes 327712 | tf_op jit(solution)/shard_map/ppermute | solution.py:28
  48.1 3.5 collective-permute-start.3
  52.9 29.1 %collective-permute-done.3 = f32[640,128]{0,1:T(8,128)S(1)} collective-permute-done((f32[640,128]{0,1:T(8,128)S(1)}, f32[640,128]{0,1:T(8,128)S(1)}, u32[]{:S(2)}, u32[]{:S(2)}) %collective-permute-start.3) | collective-permute-done | bytes 327712 | tf_op jit(solution)/shard_map/ppermute | solution.py:28
  82.8 60.2 %all-gather.10.cloned.1.call-done = bf16[10240,128]{0,1:T(8,128)(2,1)} async-done(((bf16[640,128]{0,1:T(8,128)(2,1)}), bf16[10240,128]{0,1:T(8,128)(2,1)}) %all-gather.10.cloned.1.call-update) | async-done | bytes 2621456 | tf_op jit(solution)/shard_map/all_gather | solution.py:11
  142.9 2.2 copy.16
  147.2 4.1 collective-permute-start.4
  153.1 3.2 collective-permute-start.5
  156.3 14.7 %collective-permute-done.5 = f32[1280,128]{0,1:T(8,128)S(1)} collective-permute-done((f32[1280,128]{0,1:T(8,128)S(1)}, f32[1280,128]{0,1:T(8,128)S(1)}, u32[]{:S(2)}, u32[]{:S(2)}) %collective-permute-start.5) | collective-permute-done | bytes 655392 | tf_op jit(solution)/shard_map/ppermute | solution.py:28
  171.0 4.2 collective-permute-start.6
  175.2 28.3 %collective-permute-done.6 = f32[1280,128]{0,1:T(8,128)S(1)} collective-permute-done((f32[1280,128]{0,1:T(8,128)S(1)}, f32[1280,128]{0,1:T(8,128)S(1)}, u32[]{:S(2)}, u32[]{:S(2)}) %collective-permute-start.6) | collective-permute-done | bytes 655392 | tf_op jit(solution)/shard_map/ppermute | solution.py:28
  203.5 7.4 collective-permute-start.7
  210.9 63.4 %collective-permute-done.7 = f32[1280,128]{0,1:T(8,128)S(1)} collective-permute-done((f32[1280,128]{0,1:T(8,128)S(1)}, f32[1280,128]{0,1:T(8,128)S(1)}, u32[]{:S(2)}, u32[]{:S(2)}) %collective-permute-start.7) | collective-permute-done | bytes 655392 | tf_op jit(solution)/shard_map/ppermute | solution.py:28
  274.4 11.1 %collective-permute-start.8 = (f32[640,128]{0,1:T(8,128)S(1)}, f32[640,128]{0,1:T(8,128)S(1)}, u32[]{:S(2)}, u32[]{:S(2)}) collective-permute-start(f32[640,128]{0,1:T(8,128)S(1)} %get-tuple-element.6), channel_id=1, source_target_pairs={{0,256},{256,0},{16,272},{272,16},{32,288},{288,32},{48,304},{304,... | collective-permute-start | bytes 983048 | tf_op jit(solution)/shard_map/ppermute | solution.py:28
  286.1 12.5 %collective-permute-done.8 = f32[640,128]{0,1:T(8,128)S(1)} collective-permute-done((f32[640,128]{0,1:T(8,128)S(1)}, f32[640,128]{0,1:T(8,128)S(1)}, u32[]{:S(2)}, u32[]{:S(2)}) %collective-permute-start.8) | collective-permute-done | bytes 327712 | tf_op jit(solution)/shard_map/ppermute | solution.py:28
  299.4 62.0 %all-gather.12.cloned.1.call-done = bf16[10240,128]{0,1:T(8,128)(2,1)} async-done(((bf16[640,128]{0,1:T(8,128)(2,1)}), bf16[10240,128]{0,1:T(8,128)(2,1)}) %all-gather.12.cloned.1.call-update) | async-done | bytes 2621456 | tf_op jit(solution)/shard_map/all_gather | solution.py:11
  361.4 2.2 copy.17
  365.2 4.1 collective-permute-start.9
  370.5 3.2 collective-permute-start.10
  373.7 7.6 collective-permute-done.10
  381.4 4.2 collective-permute-start.11
  385.6 14.2 %collective-permute-done.11 = f32[640,128]{0,1:T(8,128)S(1)} collective-permute-done((f32[640,128]{0,1:T(8,128)S(1)}, f32[640,128]{0,1:T(8,128)S(1)}, u32[]{:S(2)}, u32[]{:S(2)}) %collective-permute-start.11) | collective-permute-done | bytes 327712 | tf_op jit(solution)/shard_map/ppermute | solution.py:28
  399.8 7.4 collective-permute-start.12
  407.2 28.2 %collective-permute-done.12 = f32[640,128]{0,1:T(8,128)S(1)} collective-permute-done((f32[640,128]{0,1:T(8,128)S(1)}, f32[640,128]{0,1:T(8,128)S(1)}, u32[]{:S(2)}, u32[]{:S(2)}) %collective-permute-start.12) | collective-permute-done | bytes 327712 | tf_op jit(solution)/shard_map/ppermute | solution.py:28
  435.4 18.2 %collective-permute-start.13 = (f32[640,128]{0,1:T(8,128)S(1)}, f32[640,128]{0,1:T(8,128)S(1)}, u32[]{:S(2)}, u32[]{:S(2)}) collective-permute-start(f32[640,128]{0,1:T(8,128)S(1)} %add.123), channel_id=1, source_target_pairs={{0,256},{256,0},{16,272},{272,16},{32,288},{288,32},{48,304},{304,... | collective-permute-start | bytes 983048 | tf_op jit(solution)/shard_map/ppermute | solution.py:28
  453.7 14.1 %collective-permute-done.13 = f32[640,128]{0,1:T(8,128)S(1)} collective-permute-done((f32[640,128]{0,1:T(8,128)S(1)}, f32[640,128]{0,1:T(8,128)S(1)}, u32[]{:S(2)}, u32[]{:S(2)}) %collective-permute-start.13) | collective-permute-done | bytes 327712 | tf_op jit(solution)/shard_map/ppermute | solution.py:28
  468.5 58.6 %all-gather.14.cloned.1.call-done = bf16[10240,128]{0,1:T(8,128)(2,1)} async-done(((bf16[640,128]{0,1:T(8,128)(2,1)}), bf16[10240,128]{0,1:T(8,128)(2,1)}) %all-gather.14.cloned.1.call-update) | async-done | bytes 2621456 | tf_op jit(solution)/shard_map/all_gather | solution.py:11
  527.1 2.2 copy.18
  531.0 4.1 collective-permute-start.14
  536.3 3.2 collective-permute-start.15
  539.5 7.6 collective-permute-done.15
  547.2 4.2 collective-permute-start.16
  551.4 14.2 %collective-permute-done.16 = f32[640,128]{0,1:T(8,128)S(1)} collective-permute-done((f32[640,128]{0,1:T(8,128)S(1)}, f32[640,128]{0,1:T(8,128)S(1)}, u32[]{:S(2)}, u32[]{:S(2)}) %collective-permute-start.16) | collective-permute-done | bytes 327712 | tf_op jit(solution)/shard_map/ppermute | solution.py:28
  565.6 7.4 collective-permute-start.17
  573.0 28.2 %collective-permute-done.17 = f32[640,128]{0,1:T(8,128)S(1)} collective-permute-done((f32[640,128]{0,1:T(8,128)S(1)}, f32[640,128]{0,1:T(8,128)S(1)}, u32[]{:S(2)}, u32[]{:S(2)}) %collective-permute-start.17) | collective-permute-done | bytes 327712 | tf_op jit(solution)/shard_map/ppermute | solution.py:28
  601.2 18.2 %collective-permute-start.18 = (f32[640,128]{0,1:T(8,128)S(1)}, f32[640,128]{0,1:T(8,128)S(1)}, u32[]{:S(2)}, u32[]{:S(2)}) collective-permute-start(f32[640,128]{0,1:T(8,128)S(1)} %add.128), channel_id=1, source_target_pairs={{0,256},{256,0},{16,272},{272,16},{32,288},{288,32},{48,304},{304,... | collective-permute-start | bytes 983048 | tf_op jit(solution)/shard_map/ppermute | solution.py:28
  619.5 14.1 %collective-permute-done.18 = f32[640,128]{0,1:T(8,128)S(1)} collective-permute-done((f32[640,128]{0,1:T(8,128)S(1)}, f32[640,128]{0,1:T(8,128)S(1)}, u32[]{:S(2)}, u32[]{:S(2)}) %collective-permute-start.18) | collective-permute-done | bytes 327712 | tf_op jit(solution)/shard_map/ppermute | solution.py:28
  634.6 69.9 %all-gather.8.cloned.1.call-done = bf16[16,640,256]{2,1,0:T(8,128)(2,1)} async-done(((bf16[1,640,256]{2,1,0:T(8,128)(2,1)}), bf16[16,640,256]{2,1,0:T(8,128)(2,1)}) %all-gather.8.cloned.1.call-update) | async-done | bytes 5242896 | tf_op jit(solution)/shard_map/all_gather | solution.py:11
  704.5 3.3 reduce_sum.51
  708.6 2.6 collective-permute-start.19
  712.5 3.2 collective-permute-start.20
  715.7 7.6 collective-permute-done.20
  723.3 4.2 collective-permute-start.21
  727.5 14.2 %collective-permute-done.21 = f32[640,128]{0,1:T(8,128)S(1)} collective-permute-done((f32[640,128]{0,1:T(8,128)S(1)}, f32[640,128]{0,1:T(8,128)S(1)}, u32[]{:S(2)}, u32[]{:S(2)}) %collective-permute-start.21) | collective-permute-done | bytes 327712 | tf_op jit(solution)/shard_map/ppermute | solution.py:28
  741.7 7.4 collective-permute-start.22
  749.1 28.2 %collective-permute-done.22 = f32[640,128]{0,1:T(8,128)S(1)} collective-permute-done((f32[640,128]{0,1:T(8,128)S(1)}, f32[640,128]{0,1:T(8,128)S(1)}, u32[]{:S(2)}, u32[]{:S(2)}) %collective-permute-start.22) | collective-permute-done | bytes 327712 | tf_op jit(solution)/shard_map/ppermute | solution.py:28
  (68 shorter events, 22.6 us)
Async XLA Ops:
  6.5 139.9 %copy-start = (bf16[1,640,640]{2,1,0:T(8,128)(2,1)S(1)}, bf16[1,640,640]{2,1,0:T(8,128)(2,1)}, u32[]{:S(2)}) copy-start(bf16[1,640,640]{2,1,0:T(8,128)(2,1)} %param.9) | copy-start | bytes 2457604
  6.5 45.1 %copy-start.4 = (s32[2,32]{1,0:T(2,128)S(1)}, s32[2,32]{1,0:T(2,128)}, u32[]{:S(2)}) copy-start(s32[2,32]{1,0:T(2,128)} %param.7) | copy-start | bytes 772
  6.5 136.4 %all-gather.10.cloned.1.call-start = ((), (), s32[]{:S(2)}) async-start(), calls=%async_computation.1 | async-start | bytes 2785280 | tf_op jit(solution)/shard_map/all_gather | solution.py:11
  7.7 10.0 %collective-permute-start = (f32[640,128]{0,1:T(8,128)S(1)}, f32[640,128]{0,1:T(8,128)S(1)}, u32[]{:S(2)}, u32[]{:S(2)}) collective-permute-start(f32[640,128]{0,1:T(8,128)S(1)} %bitcast_convert_fusion), channel_id=1, source_target_pairs={{0,16},{16,0},{32,48},{48,32},{64,80},{80,64},{96,112},{112,96},{1... | collective-permute-start | bytes 983048 | tf_op jit(solution)/shard_map/ppermute | solution.py:28
  17.8 10.8 %collective-permute-start.1 = (f32[640,128]{0,1:T(8,128)S(1)}, f32[640,128]{0,1:T(8,128)S(1)}, u32[]{:S(2)}, u32[]{:S(2)}) collective-permute-start(f32[640,128]{0,1:T(8,128)S(1)} %fusion.24), channel_id=1, source_target_pairs={{0,32},{32,0},{16,48},{48,16},{64,96},{96,64},{80,112},{112,80},{1... | collective-permute-start | bytes 983048 | tf_op jit(solution)/shard_map/ppermute | solution.py:28
  28.6 19.4 %collective-permute-start.2 = (f32[640,128]{0,1:T(8,128)S(1)}, f32[640,128]{0,1:T(8,128)S(1)}, u32[]{:S(2)}, u32[]{:S(2)}) collective-permute-start(f32[640,128]{0,1:T(8,128)S(1)} %add.109), channel_id=1, source_target_pairs={{0,64},{64,0},{16,80},{80,16},{32,96},{96,32},{48,112},{112,48},{1... | collective-permute-start | bytes 983048 | tf_op jit(solution)/shard_map/ppermute | solution.py:28
  48.1 33.9 %collective-permute-start.3 = (f32[640,128]{0,1:T(8,128)S(1)}, f32[640,128]{0,1:T(8,128)S(1)}, u32[]{:S(2)}, u32[]{:S(2)}) collective-permute-start(f32[640,128]{0,1:T(8,128)S(1)} %add.110), channel_id=1, source_target_pairs={{0,128},{128,0},{16,144},{144,16},{32,160},{160,32},{48,176},{176,... | collective-permute-start | bytes 983048 | tf_op jit(solution)/shard_map/ppermute | solution.py:28
  82.7 278.6 %all-gather.12.cloned.1.call-start = ((), (), s32[]{:S(2)}) async-start(), calls=%async_computation.2 | async-start | bytes 2785280 | tf_op jit(solution)/shard_map/all_gather | solution.py:11
  145.2 1.7 copy-start.1
  147.2 5.8 collective-permute-start.4
  153.1 17.8 %collective-permute-start.5 = (f32[1280,128]{0,1:T(8,128)S(1)}, f32[1280,128]{0,1:T(8,128)S(1)}, u32[]{:S(2)}, u32[]{:S(2)}) collective-permute-start(f32[1280,128]{0,1:T(8,128)S(1)} %fusion.31), channel_id=1, source_target_pairs={{0,32},{32,0},{16,48},{48,16},{64,96},{96,64},{80,112},{112,80},{1... | collective-permute-start | bytes 1966088 | tf_op jit(solution)/shard_map/ppermute | solution.py:28
  171.0 32.4 %collective-permute-start.6 = (f32[1280,128]{0,1:T(8,128)S(1)}, f32[1280,128]{0,1:T(8,128)S(1)}, u32[]{:S(2)}, u32[]{:S(2)}) collective-permute-start(f32[1280,128]{0,1:T(8,128)S(1)} %add.113), channel_id=1, source_target_pairs={{0,64},{64,0},{16,80},{80,16},{32,96},{96,32},{48,112},{112,48},{1... | collective-permute-start | bytes 1966088 | tf_op jit(solution)/shard_map/ppermute | solution.py:28
  203.5 70.8 %collective-permute-start.7 = (f32[1280,128]{0,1:T(8,128)S(1)}, f32[1280,128]{0,1:T(8,128)S(1)}, u32[]{:S(2)}, u32[]{:S(2)}) collective-permute-start(f32[1280,128]{0,1:T(8,128)S(1)} %add.114), channel_id=1, source_target_pairs={{0,128},{128,0},{16,144},{144,16},{32,160},{160,32},{48,176},{176,... | collective-permute-start | bytes 1966088 | tf_op jit(solution)/shard_map/ppermute | solution.py:28
  274.4 24.2 %collective-permute-start.8 = (f32[640,128]{0,1:T(8,128)S(1)}, f32[640,128]{0,1:T(8,128)S(1)}, u32[]{:S(2)}, u32[]{:S(2)}) collective-permute-start(f32[640,128]{0,1:T(8,128)S(1)} %get-tuple-element.6), channel_id=1, source_target_pairs={{0,256},{256,0},{16,272},{272,16},{32,288},{288,32},{48,304},{304,... | collective-permute-start | bytes 983048 | tf_op jit(solution)/shard_map/ppermute | solution.py:28
  299.3 227.8 %all-gather.14.cloned.1.call-start = ((), (), s32[]{:S(2)}) async-start(), calls=%async_computation.3 | async-start | bytes 2785280 | tf_op jit(solution)/shard_map/all_gather | solution.py:11
  365.2 5.3 collective-permute-start.9
  370.5 10.8 %collective-permute-start.10 = (f32[640,128]{0,1:T(8,128)S(1)}, f32[640,128]{0,1:T(8,128)S(1)}, u32[]{:S(2)}, u32[]{:S(2)}) collective-permute-start(f32[640,128]{0,1:T(8,128)S(1)} %add.120), channel_id=1, source_target_pairs={{0,32},{32,0},{16,48},{48,16},{64,96},{96,64},{80,112},{112,80},{1... | collective-permute-start | bytes 983048 | tf_op jit(solution)/shard_map/ppermute | solution.py:28
  381.4 18.4 %collective-permute-start.11 = (f32[640,128]{0,1:T(8,128)S(1)}, f32[640,128]{0,1:T(8,128)S(1)}, u32[]{:S(2)}, u32[]{:S(2)}) collective-permute-start(f32[640,128]{0,1:T(8,128)S(1)} %add.121), channel_id=1, source_target_pairs={{0,64},{64,0},{16,80},{80,16},{32,96},{96,32},{48,112},{112,48},{1... | collective-permute-start | bytes 983048 | tf_op jit(solution)/shard_map/ppermute | solution.py:28
  399.8 35.6 %collective-permute-start.12 = (f32[640,128]{0,1:T(8,128)S(1)}, f32[640,128]{0,1:T(8,128)S(1)}, u32[]{:S(2)}, u32[]{:S(2)}) collective-permute-start(f32[640,128]{0,1:T(8,128)S(1)} %add.122), channel_id=1, source_target_pairs={{0,128},{128,0},{16,144},{144,16},{32,160},{160,32},{48,176},{176,... | collective-permute-start | bytes 983048 | tf_op jit(solution)/shard_map/ppermute | solution.py:28
  435.4 32.3 %collective-permute-start.13 = (f32[640,128]{0,1:T(8,128)S(1)}, f32[640,128]{0,1:T(8,128)S(1)}, u32[]{:S(2)}, u32[]{:S(2)}) collective-permute-start(f32[640,128]{0,1:T(8,128)S(1)} %add.123), channel_id=1, source_target_pairs={{0,256},{256,0},{16,272},{272,16},{32,288},{288,32},{48,304},{304,... | collective-permute-start | bytes 983048 | tf_op jit(solution)/shard_map/ppermute | solution.py:28
  468.5 236.0 %all-gather.8.cloned.1.call-start = ((), (), s32[]{:S(2)}) async-start(), calls=%async_computation | async-start | bytes 5570560 | tf_op jit(solution)/shard_map/all_gather | solution.py:11
  529.4 1.3 copy-start.2
  531.0 5.3 collective-permute-start.14
  536.3 10.8 %collective-permute-start.15 = (f32[640,128]{0,1:T(8,128)S(1)}, f32[640,128]{0,1:T(8,128)S(1)}, u32[]{:S(2)}, u32[]{:S(2)}) collective-permute-start(f32[640,128]{0,1:T(8,128)S(1)} %add.125), channel_id=1, source_target_pairs={{0,32},{32,0},{16,48},{48,16},{64,96},{96,64},{80,112},{112,80},{1... | collective-permute-start | bytes 983048 | tf_op jit(solution)/shard_map/ppermute | solution.py:28
  547.2 18.4 %collective-permute-start.16 = (f32[640,128]{0,1:T(8,128)S(1)}, f32[640,128]{0,1:T(8,128)S(1)}, u32[]{:S(2)}, u32[]{:S(2)}) collective-permute-start(f32[640,128]{0,1:T(8,128)S(1)} %add.126), channel_id=1, source_target_pairs={{0,64},{64,0},{16,80},{80,16},{32,96},{96,32},{48,112},{112,48},{1... | collective-permute-start | bytes 983048 | tf_op jit(solution)/shard_map/ppermute | solution.py:28
  565.6 35.6 %collective-permute-start.17 = (f32[640,128]{0,1:T(8,128)S(1)}, f32[640,128]{0,1:T(8,128)S(1)}, u32[]{:S(2)}, u32[]{:S(2)}) collective-permute-start(f32[640,128]{0,1:T(8,128)S(1)} %add.127), channel_id=1, source_target_pairs={{0,128},{128,0},{16,144},{144,16},{32,160},{160,32},{48,176},{176,... | collective-permute-start | bytes 983048 | tf_op jit(solution)/shard_map/ppermute | solution.py:28
  601.2 32.3 %collective-permute-start.18 = (f32[640,128]{0,1:T(8,128)S(1)}, f32[640,128]{0,1:T(8,128)S(1)}, u32[]{:S(2)}, u32[]{:S(2)}) collective-permute-start(f32[640,128]{0,1:T(8,128)S(1)} %add.128), channel_id=1, source_target_pairs={{0,256},{256,0},{16,272},{272,16},{32,288},{288,32},{48,304},{304,... | collective-permute-start | bytes 983048 | tf_op jit(solution)/shard_map/ppermute | solution.py:28
  634.6 73.6 %copy-start.3 = (bf16[1,640,640]{2,1,0:T(8,128)(2,1)S(1)}, bf16[1,640,640]{2,1,0:T(8,128)(2,1)}, u32[]{:S(2)}) copy-start(bf16[1,640,640]{2,1,0:T(8,128)(2,1)} %param.11) | copy-start | bytes 2457604
  708.6 3.8 collective-permute-start.19
  712.5 10.8 %collective-permute-start.20 = (f32[640,128]{0,1:T(8,128)S(1)}, f32[640,128]{0,1:T(8,128)S(1)}, u32[]{:S(2)}, u32[]{:S(2)}) collective-permute-start(f32[640,128]{0,1:T(8,128)S(1)} %add.130), channel_id=1, source_target_pairs={{0,32},{32,0},{16,48},{48,16},{64,96},{96,64},{80,112},{112,80},{1... | collective-permute-start | bytes 983048 | tf_op jit(solution)/shard_map/ppermute | solution.py:28
  723.3 18.4 %collective-permute-start.21 = (f32[640,128]{0,1:T(8,128)S(1)}, f32[640,128]{0,1:T(8,128)S(1)}, u32[]{:S(2)}, u32[]{:S(2)}) collective-permute-start(f32[640,128]{0,1:T(8,128)S(1)} %add.131), channel_id=1, source_target_pairs={{0,64},{64,0},{16,80},{80,16},{32,96},{96,32},{48,112},{112,48},{1... | collective-permute-start | bytes 983048 | tf_op jit(solution)/shard_map/ppermute | solution.py:28
  741.7 35.6 %collective-permute-start.22 = (f32[640,128]{0,1:T(8,128)S(1)}, f32[640,128]{0,1:T(8,128)S(1)}, u32[]{:S(2)}, u32[]{:S(2)}) collective-permute-start(f32[640,128]{0,1:T(8,128)S(1)} %add.132), channel_id=1, source_target_pairs={{0,128},{128,0},{16,144},{144,16},{32,160},{160,32},{48,176},{176,... | collective-permute-start | bytes 983048 | tf_op jit(solution)/shard_map/ppermute | solution.py:28
Sparse Core Ops, SparseCore 0:
  82.8 60.0 all-gather.9
  299.4 61.8 all-gather.11
  468.6 58.4 all-gather.13
  634.7 69.7 all-gather.7
